TPU v7x, 32 devices: a whole 2x2x4 slice. The times are simulated.
32 devices in a mesh: grp: 2 (over x), smp: 16 (over z, y, core).
Axes of the slice: x: 2, y: 2, z: 4, core: 2. Of those that a mesh axis runs over, the one named last changes fastest.
Arguments:
- dosage: bfloat16 [2048, 4096], P('smp', 'grp'), parts along dimension 1, may hold values from 0.008 to 4.5, as said below
- flags: int32 [256], P('grp'), parts along dimension 0, may hold values from 0 to 2047, as said below
- events: int32 [2048, 32], P('smp', 'grp'), parts along dimension 1, may hold values from 0 to 1, as said below
- offsets: float32 [2048, 32], P('smp', 'grp'), parts along dimension 1, may hold values from -3 to 3
Outputs:
- effect: float32 [16, 256], P(None, 'grp'), parts along dimension 1
- zscore: float32 [16, 256], P(None, 'grp'), parts along dimension 1
There are 2 independent parts, one for each index of `grp`. A program takes and returns all parts, laid end to end along the dimension named above; each array names one. Nothing has to cross between parts.
Inputs may be any that keep to these rules, and one draw needn't show every extreme that they name: `flags`: 128 distinct column numbers in rising order, the first 0 and the last 2047. `events`: 0 or 1; every endpoint has an event at the first sample. `dosage`: positive dosages.
All inputs are finite; a program needn't handle non-finite values.
Results may differ from a plain program's by a relative error of at most 0.0013.
Values sent between devices are 32-bit elements; how exact they have to be, the bound alone decides.
A program may use at most 64 MiB of HBM per device.

v0:
```python
import jax
import jax.numpy as jnp
from jax import lax
from jax.sharding import PartitionSpec as P

ITERS = 3


def body(dosage, flags, events, offsets):
    genotype = jnp.take(dosage, flags, axis=1).astype(jnp.float32)
    dose = genotype[:, None, :]
    hazard_offset = offsets[:, :, None]
    mark = events.astype(jnp.float32)[:, :, None]
    endpoints = offsets.shape[1]
    variants = flags.shape[0]
    effect = jnp.zeros((endpoints, variants), jnp.float32)
    zscore = effect
    for sweep in range(ITERS):
        weight = jnp.exp(hazard_offset + effect[None] * dose)
        moments = jnp.stack(
            [weight, weight * dose, weight * dose * dose, weight * dose * dose * dose]
        )
        local_suffix = lax.cumsum(moments, axis=1, reverse=True)
        totals = local_suffix[:, 0]
        every = lax.all_gather(totals[None], "smp", axis=0, tiled=True)
        pieces = every.shape[0]
        later_mask = (jnp.arange(pieces, dtype=jnp.int32) > lax.axis_index("smp")).astype(
            jnp.float32
        )
        carry = jnp.tensordot(later_mask, every, axes=1, precision=lax.Precision.HIGHEST)
        suffix = local_suffix + carry[:, None]
        first = suffix[1] / suffix[0]
        second = suffix[2] / suffix[0]
        third = suffix[3] / suffix[0]
        score = jnp.sum(mark * (dose - first), axis=0)
        information = jnp.sum(mark * (second - first * first), axis=0)
        skewness = jnp.sum(
            mark * (third - 3.0 * first * second + 2.0 * first * first * first), axis=0
        )
        score, information, skewness = lax.psum((score, information, skewness), "smp")
        effect = effect + (score + 0.5 * skewness / information) / information
        zscore = effect * jnp.sqrt(information)
    return (effect, zscore)


def solution(mesh):
    return jax.shard_map(
        body,
        mesh=mesh,
        in_specs=(P("smp", "grp"), P("grp"), P("smp", "grp"), P("smp", "grp")),
        out_specs=(P(None, "grp"), P(None, "grp")),
        check_vma=False,
    )
```

profile of v0, /device:TPU:0, one launch (start us, length us, event | category | flops | bytes accessed | tf_op | source)
XLA Modules:
  0.0 278.3 jit_solution(3950948647275496793)
XLA Ops:
  0.6 0.7 compare_and_fusion
  1.3 0.7 compare_select_fusion
  2.0 0.7 convert_element_type.13
  2.7 0.1 copy.12
  2.8 0.8 copy.15
  3.6 1.3 copy.13
  4.9 0.7 gather_fusion
  5.7 0.1 copy.16
  5.8 0.1 convert_bitcast_fusion
  5.9 0.1 copy.14
  6.0 0.4 broadcast_multiply_fusion.8
  6.4 8.6 %fusion = f32[4,128,16,128]{3,2,1,0:T(8,128)S(1)} fusion(f32[1,128,16,128]{3,2,1,0:T(8,128)S(1)} %get-tuple-element.24, f32[1,128,16,128]{3,2,1,0:T(8,128)S(1)} %get-tuple-element.23, f32[1,128,16,128]{3,2,1,0:T(8,128)S(1)} %get-tuple-element.22, f32[1,128,16,128]{3,2,1,0:T(8,128)S(1)} %get-tuple-element.33), kind=kOutput, calls=%fused_computation.1 | output fusion | flops 136314880 | bytes 8388608 | tf_op jit(solution)/shard_map/body/reduce_window_sum | solution.py:23
  15.0 24.6 %all-gather = f32[64,1,16,128]{3,2,1,0:T(8,128)S(1)} all-gather(f32[4,1,16,128]{3,2,1,0:T(8,128)S(1)} %slice.68), channel_id=2, replica_groups=mesh['grp'=2,'smp'=16] {'smp'}, dimensions={0}, use_global_device_ids=true | all-gather | bytes 557056 | tf_op jit(solution)/shard_map/all_gather | solution.py:25
  39.6 0.6 fusion.49
  40.2 0.3 broadcast_add_fusion.2
  40.5 0.8 fusion.26
  41.3 57.8 %all-reduce.2 = (f32[16,128]{1,0:T(8,128)S(1)}, f32[16,128]{1,0:T(8,128)S(1)}, f32[16,128]{1,0:T(8,128)S(1)}) all-reduce(f32[16,128]{1,0:T(8,128)S(1)} %get-tuple-element.7, f32[16,128]{1,0:T(8,128)S(1)} %get-tuple-element.10, f32[16,128]{1,0:T(8,128)S(1)} %get-tuple-element.6), channel_id=1, replica_groups=mesh['grp'=2,'smp'=16] {'smp'}, use_global_device_ids=true, to_apply=%region_6.7 | all-reduce | flops 6144 | bytes 49152 | tf_op jit(solution)/shard_map/psum | solution.py:40
  99.1 0.4 add_exponential_fusion.1
  99.5 8.6 %fusion.8 = f32[4,128,16,128]{3,2,1,0:T(8,128)S(1)} fusion(f32[1,128,16,128]{3,2,1,0:T(8,128)S(1)} %get-tuple-element.31, f32[1,128,16,128]{3,2,1,0:T(8,128)S(1)} %get-tuple-element.30, f32[1,128,16,128]{3,2,1,0:T(8,128)S(1)} %get-tuple-element.32, f32[1,128,16,128]{3,2,1,0:T(8,128)S(1)} %get-tuple-element.29), kind=kOutput, calls=%fused_computation.9 | output fusion | flops 136314880 | bytes 8388608 | tf_op jit(solution)/shard_map/body/reduce_window_sum | solution.py:23
  108.1 18.7 %all-gather.1 = f32[64,1,16,128]{3,2,1,0:T(8,128)S(1)} all-gather(f32[4,1,16,128]{3,2,1,0:T(8,128)S(1)} %slice.73), channel_id=3, replica_groups=mesh['grp'=2,'smp'=16] {'smp'}, dimensions={0}, use_global_device_ids=true | all-gather | bytes 557056 | tf_op jit(solution)/shard_map/all_gather | solution.py:25
  126.8 0.6 fusion.47
  127.4 0.3 broadcast_add_fusion.1
  127.7 0.8 fusion.29
  128.5 59.9 %all-reduce.1 = (f32[16,128]{1,0:T(8,128)S(1)}, f32[16,128]{1,0:T(8,128)S(1)}, f32[16,128]{1,0:T(8,128)S(1)}) all-reduce(f32[16,128]{1,0:T(8,128)S(1)} %get-tuple-element.5, f32[16,128]{1,0:T(8,128)S(1)} %get-tuple-element.9, f32[16,128]{1,0:T(8,128)S(1)} %get-tuple-element.4), channel_id=1, replica_groups=mesh['grp'=2,'smp'=16] {'smp'}, use_global_device_ids=true, to_apply=%region_13.14 | all-reduce | flops 6144 | bytes 49152 | tf_op jit(solution)/shard_map/psum | solution.py:40
  188.4 0.4 add_exponential_fusion
  188.8 8.6 %fusion.16 = f32[4,128,16,128]{3,2,1,0:T(8,128)S(1)} fusion(f32[1,128,16,128]{3,2,1,0:T(8,128)S(1)} %get-tuple-element.27, f32[1,128,16,128]{3,2,1,0:T(8,128)S(1)} %get-tuple-element.26, f32[1,128,16,128]{3,2,1,0:T(8,128)S(1)} %get-tuple-element.28, f32[1,128,16,128]{3,2,1,0:T(8,128)S(1)} %get-tuple-element.25), kind=kOutput, calls=%fused_computation.17 | output fusion | flops 136314880 | bytes 8388608 | tf_op jit(solution)/shard_map/body/reduce_window_sum | solution.py:23
  197.4 18.7 %all-gather.2 = f32[64,1,16,128]{3,2,1,0:T(8,128)S(1)} all-gather(f32[4,1,16,128]{3,2,1,0:T(8,128)S(1)} %slice.78), channel_id=4, replica_groups=mesh['grp'=2,'smp'=16] {'smp'}, dimensions={0}, use_global_device_ids=true | all-gather | bytes 557056 | tf_op jit(solution)/shard_map/all_gather | solution.py:25
  216.1 0.6 fusion.45
  216.7 0.3 broadcast_add_fusion
  217.0 0.8 fusion.32
  217.8 59.9 %all-reduce = (f32[16,128]{1,0:T(8,128)S(1)}, f32[16,128]{1,0:T(8,128)S(1)}, f32[16,128]{1,0:T(8,128)S(1)}) all-reduce(f32[16,128]{1,0:T(8,128)S(1)} %get-tuple-element.3, f32[16,128]{1,0:T(8,128)S(1)} %get-tuple-element.8, f32[16,128]{1,0:T(8,128)S(1)} %get-tuple-element.2), channel_id=1, replica_groups=mesh['grp'=2,'smp'=16] {'smp'}, use_global_device_ids=true, to_apply=%region_20.21 | all-reduce | flops 6144 | bytes 49152 | tf_op jit(solution)/shard_map/psum | solution.py:40
  277.7 0.6 sqrt_multiply_fusion
  (7 shorter events, 0.1 us)
where the time goes:
time: 279 us; the launch traced here: 278 us
  blocking collectives  240 us (86%)
  other arithmetic  32.9 us (12%)
  local copies, waits for them, and re-layouts  3.11 us (1%)
    psum x3, blocking collectives, body(): lax.psum((score, information, skewness), 'smp')  178 us
    all_gather x3, blocking collectives, body(): every = lax.all_gather(totals[None], 'smp', axis=0, tiled=True)  62 us
    another operation x3, other arithmetic, body(): local_suffix = lax.cumsum(moments, axis=1, reverse=True)  25.8 us

commit v1 on v0

v1 whole, which is shorter than its diff:
```python
import functools

import jax
import jax.numpy as jnp
from jax import lax
from jax.experimental import pallas as pl
from jax.experimental.pallas import tpu as pltpu
from jax.sharding import PartitionSpec as P

ITERS = 3
SUB = 8
MESH = pl.DeviceIdType.MESH
F32 = jnp.float32
BF16 = jnp.bfloat16


def thirds(x):
    high = x.astype(BF16).astype(F32)
    rest = x - high
    middle = rest.astype(BF16).astype(F32)
    return high, middle, rest - middle


def transposed_dot(a, b):
    return lax.dot_general(a, b, (((0,), (0,)), ((), ())), preferred_element_type=F32)


def iota(shape, dim):
    return lax.broadcasted_iota(jnp.int32, shape, dim)


def kernel(
    n, flags_hbm, dosage_hbm, offsets_hbm, events_hbm, effect_ref, zscore_ref,
    flags_ref, dosage_ref, offsets_ref, events_ref,
    gsend, osend, grecv, orecv, dose_ref, shift_ref, mark_ref, weight_ref, totals, carries, rsend, rrecv,
    load_sem, gsend_sem, grecv_sem, osend_sem, orecv_sem, rsend_sem, rrecv_sem,
):
    me = lax.axis_index("smp")
    rows, columns = dosage_ref.shape
    endpoints = offsets_ref.shape[1]
    variants = flags_ref.shape[1]
    own = variants // n
    lanes = dose_ref.shape[1]
    steps = rows // SUB

    loads = [
        pltpu.make_async_copy(src, dst, load_sem.at[at])
        for at, (src, dst) in enumerate(
            ((flags_hbm, flags_ref), (dosage_hbm, dosage_ref), (offsets_hbm, offsets_ref), (events_hbm, events_ref))
        )
    ]
    for load in loads:
        load.start()

    barrier = pltpu.get_barrier_semaphore()

    def peer(step):
        return lax.rem(me + step, n)

    @pl.loop(1, n)
    def _(step):
        pl.semaphore_signal(barrier, inc=1, device_id={"smp": peer(step)}, device_id_type=MESH)

    line = iota((rows, rows), 1)
    order = (iota((rows, rows), 0) == lax.rem(line, SUB) * steps + lax.div(line, SUB)).astype(F32).astype(BF16)

    loads[2].wait()
    loads[3].wait()
    three = [transposed_dot(part.astype(BF16), order) for part in thirds(offsets_ref[...])]
    osend[pl.ds(0, endpoints), :] = (three[0] + three[1]) + three[2]
    osend[pl.ds(endpoints, endpoints), :] = transposed_dot(events_ref[...].astype(F32).astype(BF16), order)

    loads[0].wait()
    loads[1].wait()
    chosen = (iota((columns, variants), 0) == flags_ref[...]).astype(F32).astype(BF16)
    genotype = jnp.dot(dosage_ref[...], chosen, preferred_element_type=F32).astype(BF16)
    gsend[...] = transposed_dot(genotype, order).reshape(n, own, rows)

    pl.semaphore_wait(barrier, n - 1)

    def gcopy(at, slot):
        return pltpu.make_async_remote_copy(
            src_ref=gsend.at[at], dst_ref=grecv.at[slot], send_sem=gsend_sem.at[at], recv_sem=grecv_sem.at[slot],
            device_id={"smp": at}, device_id_type=MESH,
        )

    def ocopy(at, slot):
        return pltpu.make_async_remote_copy(
            src_ref=osend, dst_ref=orecv.at[slot], send_sem=osend_sem.at[at], recv_sem=orecv_sem.at[slot],
            device_id={"smp": at}, device_id_type=MESH,
        )

    def rcopy(at, slot):
        return pltpu.make_async_remote_copy(
            src_ref=rsend, dst_ref=rrecv.at[slot], send_sem=rsend_sem.at[at], recv_sem=rrecv_sem.at[slot],
            device_id={"smp": at}, device_id_type=MESH,
        )

    @pl.loop(1, n)
    def _(step):
        ocopy(peer(step), me).start()
        gcopy(peer(step), me).start()

    lane_e = iota((endpoints, lanes), 1)
    spread_e = (lax.div(lane_e, own) == iota((endpoints, lanes), 0)).astype(F32).astype(BF16)
    lane_v = iota((own, lanes), 1)
    spread_v = jnp.logical_and(lax.rem(lane_v, own) == iota((own, lanes), 0), lane_v < own * endpoints)
    spread_v = spread_v.astype(F32).astype(BF16)

    def expand(slot, doses, samples):
        at = pl.ds(pl.multiple_of(slot * rows, rows), rows)
        dose_ref[at, :] = transposed_dot(doses.astype(BF16), spread_v)
        parts = [transposed_dot(part.astype(BF16), spread_e) for part in thirds(samples[:endpoints])]
        shift_ref[at, :] = (parts[0] + parts[1]) + parts[2]
        mark_ref[at, :] = transposed_dot(samples[endpoints:].astype(BF16), spread_e)

    expand(me, gsend[me], osend[...])

    @pl.loop(1, n)
    def _(step):
        slot = peer(step)
        ocopy(slot, slot).wait_recv()
        gcopy(slot, slot).wait_recv()
        expand(slot, grecv[slot], orecv[slot])

    blocks = n * SUB
    after = (iota((blocks, blocks), 1) > iota((blocks, blocks), 0)).astype(F32).astype(BF16)
    effect = jnp.zeros((1, lanes), F32)
    zscore = effect
    for sweep in range(ITERS):
        slope = jnp.broadcast_to(effect, (SUB, lanes))

        def add_up(block, _):
            sums = [jnp.zeros((SUB, lanes), F32)] * 4
            for t in range(steps):
                at = pl.ds(pl.multiple_of(block * rows + t * SUB, SUB), SUB)
                dose = dose_ref[at, :]
                moment = jnp.exp(shift_ref[at, :] + slope * dose)
                weight_ref[at, :] = moment
                for k in range(4):
                    sums[k] = sums[k] + moment
                    if k < 3:
                        moment = moment * dose
            for k in range(4):
                totals[pl.ds(pl.multiple_of(block * SUB, SUB), SUB), pl.ds(k * lanes, lanes)] = sums[k]
            return 0

        lax.fori_loop(0, n, add_up, 0, unroll=2)
        parts = [
            jnp.dot(after, part.astype(BF16), preferred_element_type=F32) for part in thirds(totals[...])
        ]
        carries[...] = (parts[0] + parts[1]) + parts[2]

        def add_terms(block, sums):
            score, information, skewness = sums
            here = pl.ds(pl.multiple_of(block * SUB, SUB), SUB)
            suffix = [carries[here, pl.ds(k * lanes, lanes)] for k in range(4)]
            for t in reversed(range(steps)):
                at = pl.ds(pl.multiple_of(block * rows + t * SUB, SUB), SUB)
                dose = dose_ref[at, :]
                mark = mark_ref[at, :]
                moment = weight_ref[at, :]
                for k in range(4):
                    suffix[k] = suffix[k] + moment
                    if k < 3:
                        moment = moment * dose
                inverse = 1.0 / suffix[0]
                first = suffix[1] * inverse
                second = suffix[2] * inverse
                third = suffix[3] * inverse
                spread = second - first * first
                score = score + mark * (dose - first)
                information = information + mark * spread
                skewness = skewness + mark * (third - first * (second + (spread + spread)))
            return score, information, skewness

        zero = jnp.zeros((SUB, lanes), F32)
        sums = lax.fori_loop(0, n, add_terms, (zero, zero, zero), unroll=2)
        score, information, skewness = (jnp.sum(x, axis=0, keepdims=True) for x in sums)
        effect = effect + (score + 0.5 * skewness / information) / information
        zscore = effect * jnp.sqrt(information)

    rsend[0:1, :] = effect
    rsend[1:2, :] = zscore

    @pl.loop(1, n)
    def _(step):
        rcopy(peer(step), me).start()

    rrecv[me] = rsend[...]

    @pl.loop(1, n)
    def _(step):
        gcopy(peer(step), me).wait_send()
        ocopy(peer(step), me).wait_send()

    @pl.loop(1, n)
    def _(step):
        rcopy(peer(step), peer(step)).wait_recv()

    owner = lax.div(iota((endpoints, lanes), 1), own) == iota((endpoints, lanes), 0)
    fold = jnp.logical_and(
        lax.rem(iota((lanes, variants), 0), own) == lax.rem(iota((lanes, variants), 1), own),
        iota((lanes, variants), 0) < own * endpoints,
    ).astype(F32).astype(BF16)
    column = lax.div(iota((endpoints, variants), 1), own)
    for which, out in enumerate((effect_ref, zscore_ref)):
        tall = jnp.concatenate([jnp.where(owner, rrecv[k, which : which + 1, :], 0.0) for k in range(n)], axis=0)
        parts = [jnp.dot(part.astype(BF16), fold, preferred_element_type=F32) for part in thirds(tall)]
        tall = (parts[0] + parts[1]) + parts[2]
        result = jnp.zeros((endpoints, variants), F32)
        for k in range(n):
            result = jnp.where(column == k, tall[k * endpoints : (k + 1) * endpoints], result)
        out[...] = result

    @pl.loop(1, n)
    def _(step):
        rcopy(peer(step), me).wait_send()


def solution(mesh):
    n = mesh.shape["smp"]

    def body(dosage, flags, events, offsets):
        rows, columns = dosage.shape
        endpoints = offsets.shape[1]
        variants = flags.shape[0]
        own = variants // n
        lanes = -(-own * endpoints // 128) * 128
        out = jax.ShapeDtypeStruct((endpoints, variants), F32)
        return pl.pallas_call(
            functools.partial(kernel, n),
            out_shape=(out, out),
            in_specs=[pl.BlockSpec(memory_space=pl.ANY)] * 4,
            out_specs=[pl.BlockSpec(memory_space=pltpu.VMEM)] * 2,
            scratch_shapes=[
                pltpu.VMEM((1, variants), jnp.int32),
                pltpu.VMEM((rows, columns), BF16),
                pltpu.VMEM((rows, endpoints), F32),
                pltpu.VMEM((rows, endpoints), jnp.int32),
                pltpu.VMEM((n, own, rows), F32),
                pltpu.VMEM((2 * endpoints, rows), F32),
                pltpu.VMEM((n, own, rows), F32),
                pltpu.VMEM((n, 2 * endpoints, rows), F32),
                pltpu.VMEM((n * rows, lanes), F32),
                pltpu.VMEM((n * rows, lanes), F32),
                pltpu.VMEM((n * rows, lanes), F32),
                pltpu.VMEM((n * rows, lanes), F32),
                pltpu.VMEM((n * SUB, 4 * lanes), F32),
                pltpu.VMEM((n * SUB, 4 * lanes), F32),
                pltpu.VMEM((2, lanes), F32),
                pltpu.VMEM((n, 2, lanes), F32),
                pltpu.SemaphoreType.DMA((4,)),
            ]
            + [pltpu.SemaphoreType.DMA((n,))] * 6,
            compiler_params=pltpu.CompilerParams(collective_id=0, has_side_effects=True),
        )(flags.reshape(1, variants), dosage, offsets, events)

    return jax.shard_map(
        body,
        mesh=mesh,
        in_specs=(P("smp", "grp"), P("grp"), P("smp", "grp"), P("smp", "grp")),
        out_specs=(P(None, "grp"), P(None, "grp")),
        check_vma=False,
    )
```

time: 279 us -> 33.5 us (0.12)
  blocking collectives: 240 us -> 0 us
  other arithmetic: 32.9 us -> 0 us
  Pallas kernels: 0 us -> 28.6 us
    psum x3 -> x0, blocking collectives: 178 us -> none  [body(): lax.psum((score, information, skewness), 'smp')]
    all_gather x3 -> x0, blocking collectives: 62 us -> none  [body(): every = lax.all_gather(totals[None], 'smp', axis=0, tiled=True)]
    pallas_call x0 -> x1, Pallas kernels: none -> 28.6 us  [body(): pl.pallas_call(functools.partial(kernel, n), out_shape=(out, out), in_spe...]
    another operation x4 -> x0, other arithmetic: 25.9 us -> none  [the longest x3 25.8 us: body(): local_suffix = lax.cumsum(moments, axis=1, reverse=True)]
where the time goes in v1:
time: 33.5 us; the launch traced here: 33.3 us
  Pallas kernels  28.6 us (85%)
  local copies, waits for them, and re-layouts  4.05 us (12%)
  between operations  0.66 us (2%)
    pallas_call x1, Pallas kernels, body(): pl.pallas_call(functools.partial(kernel, n), out_shape=(out, out), in_spe...  28.6 us
    unnamed x8, local copies, waits for them, and re-layouts  4.05 us

profile of v1, /device:TPU:0, one launch (start us, length us, event | category | flops | bytes accessed | tf_op | source)
XLA Modules:
  0.0 33.3 jit_solution(12857288766846783872)
XLA Ops:
  0.6 0.0 copy-start
  0.6 1.4 %copy.7.events_hbm = s32[128,16]{1,0:T(8,128)} copy(s32[128,16]{0,1:T(8,128)} %param.6) | data formatting | bytes 16384 | tf_op args[2]
  2.1 0.0 copy-done
  2.1 0.7 %copy.6.offsets_hbm = f32[128,16]{1,0:T(8,128)} copy(f32[128,16]{0,1:T(8,128)S(1)} %copy-done) | data formatting | bytes 16384 | tf_op args[3]
  2.8 28.6 %shard_map.59 = (f32[16,128]{1,0:T(8,128)}, f32[16,128]{1,0:T(8,128)}) custom-call(s32[1,128]{1,0:T(1,128)} %bitcast.1, bf16[128,2048]{1,0:T(8,128)(2,1)} %dosage_hbm.1, f32[128,16]{1,0:T(8,128)} %copy.6.offsets_hbm, s32[128,16]{1,0:T(8,128)} %copy.7.events_hbm), custom_call_target="tpu_custom_call" | custom-call | tf_op jit(solution)/shard_map/pallas_call | solution.py:231
  31.4 0.0 copy-start.1
  31.4 1.3 %copy.10 = f32[16,128]{1,0:T(8,128)} copy(f32[16,128]{1,0:T(8,128)} %get-tuple-element.4) | data formatting | bytes 16384
  32.7 0.0 copy-done.1
  32.7 0.6 %copy.11 = f32[16,128]{1,0:T(8,128)} copy(f32[16,128]{1,0:T(8,128)S(1)} %copy-done.1) | data formatting | bytes 16384
Async XLA Ops:
  0.6 1.4 %copy-start = (f32[128,16]{0,1:T(8,128)S(1)}, f32[128,16]{0,1:T(8,128)}, u32[]{:S(2)}) copy-start(f32[128,16]{0,1:T(8,128)} %param.7) | copy-start | bytes 24580
  31.4 1.3 %copy-start.1 = (f32[16,128]{1,0:T(8,128)S(1)}, f32[16,128]{1,0:T(8,128)}, u32[]{:S(2)}) copy-start(f32[16,128]{1,0:T(8,128)} %get-tuple-element.5) | copy-start | bytes 24580

commit v2 on v1

--- a/solution.py
+++ b/solution.py
@@ -37,7 +37,7 @@
 ):
     me = lax.axis_index("smp")
     rows, columns = dosage_ref.shape
-    endpoints = offsets_ref.shape[1]
+    endpoints = offsets_ref.shape[0]
     variants = flags_ref.shape[1]
     own = variants // n
     lanes = dose_ref.shape[1]
@@ -66,13 +66,15 @@
 
     loads[2].wait()
     loads[3].wait()
-    three = [transposed_dot(part.astype(BF16), order) for part in thirds(offsets_ref[...])]
-    osend[pl.ds(0, endpoints), :] = (three[0] + three[1]) + three[2]
-    osend[pl.ds(endpoints, endpoints), :] = transposed_dot(events_ref[...].astype(F32).astype(BF16), order)
+    four = jnp.concatenate([*thirds(offsets_ref[...]), events_ref[...].astype(F32)], axis=0)
+    four = jnp.dot(four.astype(BF16), order, preferred_element_type=F32)
+    high, middle, low, events = (four[k * endpoints : (k + 1) * endpoints] for k in range(4))
+    osend[pl.ds(0, endpoints), :] = (high + middle) + low
+    osend[pl.ds(endpoints, endpoints), :] = events
 
     loads[0].wait()
+    chosen = (iota((columns, variants), 0) == flags_ref[...]).astype(F32).astype(BF16)
     loads[1].wait()
-    chosen = (iota((columns, variants), 0) == flags_ref[...]).astype(F32).astype(BF16)
     genotype = jnp.dot(dosage_ref[...], chosen, preferred_element_type=F32).astype(BF16)
     gsend[...] = transposed_dot(genotype, order).reshape(n, own, rows)
 
@@ -84,9 +86,10 @@
             device_id={"smp": at}, device_id_type=MESH,
         )
 
-    def ocopy(at, slot):
+    def ocopy(at, slot, src=osend, relayed=0):
+        mark = n + slot if relayed else at
         return pltpu.make_async_remote_copy(
-            src_ref=osend, dst_ref=orecv.at[slot], send_sem=osend_sem.at[at], recv_sem=orecv_sem.at[slot],
+            src_ref=src, dst_ref=orecv.at[slot], send_sem=osend_sem.at[mark], recv_sem=orecv_sem.at[slot],
             device_id={"smp": at}, device_id_type=MESH,
         )
 
@@ -96,32 +99,64 @@
             device_id={"smp": at}, device_id_type=MESH,
         )
 
-    @pl.loop(1, n)
-    def _(step):
-        ocopy(peer(step), me).start()
-        gcopy(peer(step), me).start()
+    half = lax.rem(me, 2)
+    other = me + 1 - 2 * half
+
+    def chip(step):
+        return lax.rem(me - half + 2 * step + n, n)
+
+    ocopy(other, me).start()
+    gcopy(other, me).start()
+
+    @pl.loop(1, n // 2)
+    def _(step):
+        at = chip(step)
+        ocopy(at + half, me).start()
+        gcopy(at + half, me).start()
+        gcopy(at + 1 - half, me).start()
 
     lane_e = iota((endpoints, lanes), 1)
-    spread_e = (lax.div(lane_e, own) == iota((endpoints, lanes), 0)).astype(F32).astype(BF16)
     lane_v = iota((own, lanes), 1)
-    spread_v = jnp.logical_and(lax.rem(lane_v, own) == iota((own, lanes), 0), lane_v < own * endpoints)
-    spread_v = spread_v.astype(F32).astype(BF16)
+    spread_e = (lax.div(lane_e, own) == iota((endpoints, lanes), 0)).astype(F32)
+    spread_v = jnp.logical_and(lax.rem(lane_v, own) == iota((own, lanes), 0), lane_v < own * endpoints).astype(F32)
+    none_e, none_v = jnp.zeros_like(spread_e), jnp.zeros_like(spread_v)
+    spread = jnp.concatenate(
+        [jnp.concatenate([spread_e, none_e, none_e], axis=1)] * 3
+        + [jnp.concatenate([none_e, spread_e, none_e], axis=1), jnp.concatenate([none_v, none_v, spread_v], axis=1)],
+        axis=0,
+    ).astype(BF16)
 
     def expand(slot, doses, samples):
         at = pl.ds(pl.multiple_of(slot * rows, rows), rows)
-        dose_ref[at, :] = transposed_dot(doses.astype(BF16), spread_v)
-        parts = [transposed_dot(part.astype(BF16), spread_e) for part in thirds(samples[:endpoints])]
-        shift_ref[at, :] = (parts[0] + parts[1]) + parts[2]
-        mark_ref[at, :] = transposed_dot(samples[endpoints:].astype(BF16), spread_e)
+        mixed = jnp.concatenate([*thirds(samples[:endpoints]), samples[endpoints:], doses], axis=0)
+        mixed = transposed_dot(mixed.astype(BF16), spread)
+        shift_ref[at, :] = mixed[:, :lanes]
+        mark_ref[at, :] = mixed[:, lanes : 2 * lanes]
+        dose_ref[at, :] = mixed[:, 2 * lanes :]
 
     expand(me, gsend[me], osend[...])
-
-    @pl.loop(1, n)
-    def _(step):
-        slot = peer(step)
-        ocopy(slot, slot).wait_recv()
-        gcopy(slot, slot).wait_recv()
-        expand(slot, grecv[slot], orecv[slot])
+    ocopy(other, other).wait_recv()
+    gcopy(other, other).wait_recv()
+    expand(other, grecv[other], orecv[other])
+
+    @pl.loop(1, n // 2)
+    def _(step):
+        near = chip(-step) + half
+        ocopy(near, near).wait_recv()
+        ocopy(other, near, orecv.at[near], 1).start()
+        gcopy(near, near).wait_recv()
+        expand(near, grecv[near], orecv[near])
+        @pl.when(step > 1)
+        def _():
+            late = chip(1 - step) + 1 - half
+            ocopy(late, late).wait_recv()
+            gcopy(late, late).wait_recv()
+            expand(late, grecv[late], orecv[late])
+
+    last = chip(1 - n // 2) + 1 - half
+    ocopy(last, last).wait_recv()
+    gcopy(last, last).wait_recv()
+    expand(last, grecv[last], orecv[last])
 
     blocks = n * SUB
     after = (iota((blocks, blocks), 1) > iota((blocks, blocks), 0)).astype(F32).astype(BF16)
@@ -188,11 +223,17 @@
         rcopy(peer(step), me).start()
 
     rrecv[me] = rsend[...]
+    ocopy(other, me).wait_send()
+
+    @pl.loop(1, n // 2)
+    def _(step):
+        near = chip(step) + half
+        ocopy(near, me).wait_send()
+        ocopy(other, near, orecv.at[near], 1).wait_send()
 
     @pl.loop(1, n)
     def _(step):
         gcopy(peer(step), me).wait_send()
-        ocopy(peer(step), me).wait_send()
 
     @pl.loop(1, n)
     def _(step):
@@ -236,8 +277,8 @@
             scratch_shapes=[
                 pltpu.VMEM((1, variants), jnp.int32),
                 pltpu.VMEM((rows, columns), BF16),
-                pltpu.VMEM((rows, endpoints), F32),
-                pltpu.VMEM((rows, endpoints), jnp.int32),
+                pltpu.VMEM((endpoints, rows), F32),
+                pltpu.VMEM((endpoints, rows), jnp.int32),
                 pltpu.VMEM((n, own, rows), F32),
                 pltpu.VMEM((2 * endpoints, rows), F32),
                 pltpu.VMEM((n, own, rows), F32),
@@ -252,9 +293,9 @@
                 pltpu.VMEM((n, 2, lanes), F32),
                 pltpu.SemaphoreType.DMA((4,)),
             ]
-            + [pltpu.SemaphoreType.DMA((n,))] * 6,
+            + [pltpu.SemaphoreType.DMA((size,)) for size in (n, n, 2 * n, n, n, n)],
             compiler_params=pltpu.CompilerParams(collective_id=0, has_side_effects=True),
-        )(flags.reshape(1, variants), dosage, offsets, events)
+        )(flags.reshape(1, variants), dosage, offsets.T, events.T)
 
     return jax.shard_map(
         body,

time: 33.5 us -> 28.5 us (0.85)
  Pallas kernels: 28.6 us -> 25.8 us
  local copies, waits for them, and re-layouts: 4.05 us -> 1.9 us
    pallas_call x1, Pallas kernels: 28.6 us -> 25.8 us  [body(): pl.pallas_call(functools.partial(kernel, n), out_shape=(out, out), in_spe...]
    unnamed x8 -> x4, local copies, waits for them, and re-layouts: 4.05 us -> 1.9 us
where the time goes in v2:
time: 28.5 us; the launch traced here: 28.3 us
  Pallas kernels  25.8 us (91%)
  local copies, waits for them, and re-layouts  1.9 us (7%)
  between operations  0.65 us (2%)
    pallas_call x1, Pallas kernels, body(): pl.pallas_call(functools.partial(kernel, n), out_shape=(out, out), in_spe...  25.8 us
    unnamed x4, local copies, waits for them, and re-layouts  1.9 us

profile of v2, /device:TPU:0, one launch (start us, length us, event | category | flops | bytes accessed | tf_op | source)
XLA Modules:
  0.0 28.3 jit_solution(11941963241204468888)
XLA Ops:
  0.6 25.8 %shard_map.59 = (f32[16,128]{1,0:T(8,128)}, f32[16,128]{1,0:T(8,128)}) custom-call(s32[1,128]{1,0:T(1,128)} %bitcast.5, bf16[128,2048]{1,0:T(8,128)(2,1)} %dosage_hbm.1, f32[16,128]{1,0:T(8,128)} %bitcast.3, s32[16,128]{1,0:T(8,128)} %bitcast.4), custom_call_target="tpu_custom_call" | custom-call | tf_op jit(solution)/shard_map/pallas_call | solution.py:272
  26.4 0.0 copy-start
  26.4 1.3 %copy.8 = f32[16,128]{1,0:T(8,128)} copy(f32[16,128]{1,0:T(8,128)} %get-tuple-element.4) | data formatting | bytes 16384
  27.7 0.0 copy-done
  27.7 0.6 %copy.9 = f32[16,128]{1,0:T(8,128)} copy(f32[16,128]{1,0:T(8,128)S(1)} %copy-done) | data formatting | bytes 16384
Async XLA Ops:
  26.4 1.3 %copy-start = (f32[16,128]{1,0:T(8,128)S(1)}, f32[16,128]{1,0:T(8,128)}, u32[]{:S(2)}) copy-start(f32[16,128]{1,0:T(8,128)} %get-tuple-element.5) | copy-start | bytes 24580

commit v3 on v1

v3 whole, which is shorter than its diff:
```python
import functools

import jax
import jax.numpy as jnp
from jax import lax
from jax.experimental import pallas as pl
from jax.experimental.pallas import tpu as pltpu
from jax.sharding import PartitionSpec as P

ITERS = 3
SUB = 8
MESH = pl.DeviceIdType.MESH
F32 = jnp.float32
BF16 = jnp.bfloat16


def thirds(x):
    high = x.astype(BF16).astype(F32)
    rest = x - high
    middle = rest.astype(BF16).astype(F32)
    return high, middle, rest - middle


def transposed_dot(a, b):
    return lax.dot_general(a, b, (((0,), (0,)), ((), ())), preferred_element_type=F32)


def iota(shape, dim):
    return lax.broadcasted_iota(jnp.int32, shape, dim)


def kernel(
    n, flags_hbm, dosage_hbm, offsets_hbm, events_hbm, out_ref,
    flags_ref, dosage_ref, offsets_ref, events_ref,
    send, recv, dose_ref, shift_ref, mark_ref, weight_ref, totals, carries, rsend, rrecv,
    load_sem, send_sem, recv_sem, rsend_sem, rrecv_sem,
):
    me = lax.axis_index("smp")
    rows, columns = dosage_ref.shape
    endpoints = offsets_ref.shape[0]
    part = endpoints // 2
    variants = flags_ref.shape[1]
    own = variants * 2 // n
    lanes = dose_ref.shape[1]
    steps = rows // SUB

    loads = [
        pltpu.make_async_copy(src, dst, load_sem.at[at])
        for at, (src, dst) in enumerate(
            ((flags_hbm, flags_ref), (dosage_hbm, dosage_ref), (offsets_hbm, offsets_ref), (events_hbm, events_ref))
        )
    ]
    for load in loads:
        load.start()

    barrier = pltpu.get_barrier_semaphore()

    def peer(step):
        return lax.rem(me + step, n)

    @pl.loop(1, n)
    def _(step):
        pl.semaphore_signal(barrier, inc=1, device_id={"smp": peer(step)}, device_id_type=MESH)

    line = iota((rows, rows), 1)
    order = (iota((rows, rows), 0) == lax.rem(line, SUB) * steps + lax.div(line, SUB)).astype(F32).astype(BF16)

    loads[2].wait()
    loads[3].wait()
    four = jnp.concatenate([*thirds(offsets_ref[...]), events_ref[...].astype(F32)], axis=0)
    four = jnp.dot(four.astype(BF16), order, preferred_element_type=F32)
    high, middle, low, events = (four[k * endpoints : (k + 1) * endpoints] for k in range(4))
    offsets = (high + middle) + low
    for k in range(n):
        for at, values in ((own, offsets), (own + part, events)):
            send[k, pl.ds(at, part), :] = values[k % 2 * part : (k % 2 + 1) * part]

    loads[0].wait()
    chosen = (iota((columns, variants), 0) == flags_ref[...]).astype(F32).astype(BF16)
    loads[1].wait()
    genotype = jnp.dot(dosage_ref[...], chosen, preferred_element_type=F32).astype(BF16)
    genotype = transposed_dot(genotype, order)
    for k in range(n):
        send[k, pl.ds(0, own), :] = genotype[k // 2 * own : (k // 2 + 1) * own]

    pl.semaphore_wait(barrier, n - 1)

    def copy(at, slot):
        return pltpu.make_async_remote_copy(
            src_ref=send.at[at], dst_ref=recv.at[slot], send_sem=send_sem.at[at], recv_sem=recv_sem.at[slot],
            device_id={"smp": at}, device_id_type=MESH,
        )

    def rcopy(at, slot):
        return pltpu.make_async_remote_copy(
            src_ref=rsend, dst_ref=rrecv.at[slot], send_sem=rsend_sem.at[at], recv_sem=rrecv_sem.at[slot],
            device_id={"smp": at}, device_id_type=MESH,
        )

    @pl.loop(1, n)
    def _(step):
        copy(peer(step), me).start()

    lane_e = iota((part, lanes), 1)
    lane_v = iota((own, lanes), 1)
    spread_e = (lax.div(lane_e, own) == iota((part, lanes), 0)).astype(F32)
    spread_v = jnp.logical_and(lax.rem(lane_v, own) == iota((own, lanes), 0), lane_v < own * part).astype(F32)
    none_e, none_v = jnp.zeros_like(spread_e), jnp.zeros_like(spread_v)
    spread = jnp.concatenate(
        [jnp.concatenate([none_v, none_v, spread_v], axis=1)]
        + [jnp.concatenate([spread_e, none_e, none_e], axis=1)] * 3
        + [jnp.concatenate([none_e, spread_e, none_e], axis=1)],
        axis=0,
    ).astype(BF16)

    def add_up(block, slope):
        sums = [jnp.zeros((SUB, lanes), F32)] * 4
        for t in range(steps):
            at = pl.ds(pl.multiple_of(block * rows + t * SUB, SUB), SUB)
            dose = dose_ref[at, :]
            moment = jnp.exp(shift_ref[at, :] if slope is None else shift_ref[at, :] + slope * dose)
            weight_ref[at, :] = moment
            for k in range(4):
                sums[k] = sums[k] + moment
                if k < 3:
                    moment = moment * dose
        for k in range(4):
            totals[pl.ds(pl.multiple_of(block * SUB, SUB), SUB), pl.ds(k * lanes, lanes)] = sums[k]

    def expand(slot, values):
        at = pl.ds(pl.multiple_of(slot * rows, rows), rows)
        doses, samples, events = values[:own], values[own : own + part], values[own + part :]
        mixed = jnp.concatenate([doses, *thirds(samples), events], axis=0)
        mixed = transposed_dot(mixed.astype(BF16), spread)
        shift_ref[at, :] = mixed[:, :lanes]
        mark_ref[at, :] = mixed[:, lanes : 2 * lanes]
        dose_ref[at, :] = mixed[:, 2 * lanes :]
        add_up(slot, None)

    expand(me, send[me])

    @pl.loop(1, n)
    def _(step):
        slot = peer(n - step)
        copy(slot, slot).wait_recv()
        expand(slot, recv[slot])

    blocks = n * SUB
    after = (iota((blocks, blocks), 1) > iota((blocks, blocks), 0)).astype(F32).astype(BF16)
    effect = jnp.zeros((1, lanes), F32)
    zscore = effect
    for sweep in range(ITERS):
        if sweep:
            slope = jnp.broadcast_to(effect, (SUB, lanes))

            def again(block, _):
                add_up(block, slope)
                return 0

            lax.fori_loop(0, n, again, 0, unroll=2)
        parts = [
            jnp.dot(after, part.astype(BF16), preferred_element_type=F32) for part in thirds(totals[...])
        ]
        carries[...] = (parts[0] + parts[1]) + parts[2]

        def add_terms(block, sums):
            score, information, skewness = sums
            here = pl.ds(pl.multiple_of(block * SUB, SUB), SUB)
            suffix = [carries[here, pl.ds(k * lanes, lanes)] for k in range(4)]
            for t in reversed(range(steps)):
                at = pl.ds(pl.multiple_of(block * rows + t * SUB, SUB), SUB)
                dose = dose_ref[at, :]
                mark = mark_ref[at, :]
                moment = weight_ref[at, :]
                for k in range(4):
                    suffix[k] = suffix[k] + moment
                    if k < 3:
                        moment = moment * dose
                inverse = 1.0 / suffix[0]
                first = suffix[1] * inverse
                second = suffix[2] * inverse
                third = suffix[3] * inverse
                spread = second - first * first
                score = score + mark * (dose - first)
                information = information + mark * spread
                skewness = skewness + mark * (third - first * (second + (spread + spread)))
            return score, information, skewness

        zero = jnp.zeros((SUB, lanes), F32)
        sums = lax.fori_loop(0, n, add_terms, (zero, zero, zero), unroll=2)
        score, information, skewness = (jnp.sum(x, axis=0, keepdims=True) for x in sums)
        effect = effect + (score + 0.5 * skewness / information) / information
        zscore = effect * jnp.sqrt(information)

    rsend[0:1, :] = effect
    rsend[1:2, :] = zscore

    @pl.loop(1, n)
    def _(step):
        rcopy(peer(step), me).start()

    rrecv[me] = rsend[...]

    @pl.loop(1, n)
    def _(step):
        copy(peer(step), me).wait_send()

    @pl.loop(1, n)
    def _(step):
        rcopy(peer(step), peer(step)).wait_recv()

    out_ref[...] = rrecv[...]

    @pl.loop(1, n)
    def _(step):
        rcopy(peer(step), me).wait_send()


def unfold(n, held, effect_ref, zscore_ref):
    endpoints, variants = effect_ref.shape
    part = endpoints // 2
    own = variants * 2 // n
    lanes = held.shape[2]
    owner = lax.div(iota((part, lanes), 1), own) == iota((part, lanes), 0)
    fold = jnp.logical_and(
        lax.rem(iota((lanes, variants), 0), own) == lax.rem(iota((lanes, variants), 1), own),
        iota((lanes, variants), 0) < own * part,
    ).astype(F32).astype(BF16)
    column = lax.div(iota((endpoints, variants), 1), own)
    for which, out in enumerate((effect_ref, zscore_ref)):
        tall = jnp.concatenate([jnp.where(owner, held[k, which : which + 1, :], 0.0) for k in range(n)], axis=0)
        parts = [jnp.dot(third.astype(BF16), fold, preferred_element_type=F32) for third in thirds(tall)]
        tall = (parts[0] + parts[1]) + parts[2]
        result = jnp.zeros((endpoints, variants), F32)
        for c in range(n // 2):
            result = jnp.where(column == c, tall[c * endpoints : (c + 1) * endpoints], result)
        out[...] = result


def solution(mesh):
    n = mesh.shape["smp"]

    def body(dosage, flags, events, offsets):
        rows, columns = dosage.shape
        endpoints = offsets.shape[1]
        variants = flags.shape[0]
        own = variants * 2 // n
        part = endpoints // 2
        lanes = -(-own * part // 128) * 128
        out = jax.ShapeDtypeStruct((endpoints, variants), F32)
        held = pl.pallas_call(
            functools.partial(kernel, n),
            out_shape=jax.ShapeDtypeStruct((n, 2, lanes), F32),
            in_specs=[pl.BlockSpec(memory_space=pl.ANY)] * 4,
            out_specs=pl.BlockSpec(memory_space=pltpu.VMEM),
            scratch_shapes=[
                pltpu.VMEM((1, variants), jnp.int32),
                pltpu.VMEM((rows, columns), BF16),
                pltpu.VMEM((endpoints, rows), F32),
                pltpu.VMEM((endpoints, rows), jnp.int32),
                pltpu.VMEM((n, own + 2 * part, rows), F32),
                pltpu.VMEM((n, own + 2 * part, rows), F32),
                pltpu.VMEM((n * rows, lanes), F32),
                pltpu.VMEM((n * rows, lanes), F32),
                pltpu.VMEM((n * rows, lanes), F32),
                pltpu.VMEM((n * rows, lanes), F32),
                pltpu.VMEM((n * SUB, 4 * lanes), F32),
                pltpu.VMEM((n * SUB, 4 * lanes), F32),
                pltpu.VMEM((2, lanes), F32),
                pltpu.VMEM((n, 2, lanes), F32),
                pltpu.SemaphoreType.DMA((4,)),
            ]
            + [pltpu.SemaphoreType.DMA((n,))] * 4,
            compiler_params=pltpu.CompilerParams(collective_id=0, has_side_effects=True),
        )(flags.reshape(1, variants), dosage, offsets.T, events.T)
        return pl.pallas_call(
            functools.partial(unfold, n),
            out_shape=(out, out),
            in_specs=[pl.BlockSpec(memory_space=pltpu.VMEM)],
            out_specs=[pl.BlockSpec(memory_space=pltpu.VMEM)] * 2,
        )(held)

    return jax.shard_map(
        body,
        mesh=mesh,
        in_specs=(P("smp", "grp"), P("grp"), P("smp", "grp"), P("smp", "grp")),
        out_specs=(P(None, "grp"), P(None, "grp")),
        check_vma=False,
    )
```

time: 33.5 us -> 27.4 us (0.82)
  local copies, waits for them, and re-layouts: 4.05 us -> 0 us
  Pallas kernels: 28.6 us -> 26.4 us
    unnamed x8 -> x0, local copies, waits for them, and re-layouts: 4.05 us -> none
    pallas_call x1 -> x2, Pallas kernels: 28.6 us -> 26.4 us  [the longest x1 24.9 us: body(): pl.pallas_call(functools.partial(kernel, n), out_shape=jax.ShapeDtypeStru...]
where the time goes in v3:
time: 27.4 us; the launch traced here: 27.1 us
  Pallas kernels  26.4 us (96%)
  between operations  0.64 us (2%)
    pallas_call x1, Pallas kernels, body(): pl.pallas_call(functools.partial(kernel, n), out_shape=jax.ShapeDtypeStru...  24.9 us
    pallas_call x1, Pallas kernels, body(): pl.pallas_call(functools.partial(unfold, n), out_shape=(out, out), in_spe...  1.53 us

profile of v3, /device:TPU:0, one launch (start us, length us, event | category | flops | bytes accessed | tf_op | source)
XLA Modules:
  0.0 27.1 jit_solution(12429872127997249020)
XLA Ops:
  0.6 24.9 %shard_map.59.held = f32[16,2,128]{2,1,0:T(2,128)} custom-call(s32[1,128]{1,0:T(1,128)} %bitcast.5, bf16[128,2048]{1,0:T(8,128)(2,1)} %dosage_hbm.1, f32[16,128]{1,0:T(8,128)} %bitcast.3, s32[16,128]{1,0:T(8,128)} %bitcast.4), custom_call_target="tpu_custom_call" | custom-call | tf_op jit(solution)/shard_map/pallas_call | solution.py:251
  25.5 1.5 %shard_map.60 = (f32[16,128]{1,0:T(8,128)}, f32[16,128]{1,0:T(8,128)}) custom-call(f32[16,2,128]{2,1,0:T(2,128)} %shard_map.59.held), custom_call_target="tpu_custom_call" | custom-call | tf_op jit(solution)/shard_map/pallas_call | solution.py:276

commit v4 on v3

--- a/solution.py
+++ b/solution.py
@@ -9,6 +9,7 @@
 
 ITERS = 3
 SUB = 8
+GROUP = 5
 MESH = pl.DeviceIdType.MESH
 F32 = jnp.float32
 BF16 = jnp.bfloat16
@@ -99,7 +100,7 @@
 
     @pl.loop(1, n)
     def _(step):
-        copy(peer(step), me).start()
+        copy(peer(lax.rem(step + n // 2 - 2, n - 1) + 1), me).start()
 
     lane_e = iota((part, lanes), 1)
     lane_v = iota((own, lanes), 1)
@@ -113,37 +114,53 @@
         axis=0,
     ).astype(BF16)
 
+    def keep(block, sums):
+        for k in range(4):
+            totals[pl.ds(pl.multiple_of(block * SUB, SUB), SUB), pl.ds(k * lanes, lanes)] = sums[k]
+
     def add_up(block, slope):
         sums = [jnp.zeros((SUB, lanes), F32)] * 4
         for t in range(steps):
             at = pl.ds(pl.multiple_of(block * rows + t * SUB, SUB), SUB)
             dose = dose_ref[at, :]
-            moment = jnp.exp(shift_ref[at, :] if slope is None else shift_ref[at, :] + slope * dose)
+            moment = jnp.exp(shift_ref[at, :] + slope * dose)
             weight_ref[at, :] = moment
             for k in range(4):
                 sums[k] = sums[k] + moment
                 if k < 3:
                     moment = moment * dose
-        for k in range(4):
-            totals[pl.ds(pl.multiple_of(block * SUB, SUB), SUB), pl.ds(k * lanes, lanes)] = sums[k]
-
-    def expand(slot, values):
-        at = pl.ds(pl.multiple_of(slot * rows, rows), rows)
-        doses, samples, events = values[:own], values[own : own + part], values[own + part :]
-        mixed = jnp.concatenate([doses, *thirds(samples), events], axis=0)
-        mixed = transposed_dot(mixed.astype(BF16), spread)
-        shift_ref[at, :] = mixed[:, :lanes]
-        mark_ref[at, :] = mixed[:, lanes : 2 * lanes]
-        dose_ref[at, :] = mixed[:, 2 * lanes :]
-        add_up(slot, None)
-
-    expand(me, send[me])
-
-    @pl.loop(1, n)
-    def _(step):
-        slot = peer(n - step)
-        copy(slot, slot).wait_recv()
-        expand(slot, recv[slot])
+        keep(block, sums)
+
+    def expand(slots, pieces):
+        mixed = []
+        for values in pieces:
+            doses, samples, events = values[:own], values[own : own + part], values[own + part :]
+            tall = jnp.concatenate([doses, *thirds(samples), events], axis=0)
+            mixed.append(transposed_dot(tall.astype(BF16), spread))
+        for slot, values in zip(slots, mixed):
+            at = pl.ds(pl.multiple_of(slot * rows, rows), rows)
+            shifts, doses = values[:, :lanes], values[:, 2 * lanes :]
+            shift_ref[at, :] = shifts
+            mark_ref[at, :] = values[:, lanes : 2 * lanes]
+            dose_ref[at, :] = doses
+            moment = jnp.exp(shifts)
+            weight_ref[at, :] = moment
+            sums = []
+            for k in range(4):
+                sums.append(jnp.sum(moment.reshape(steps, SUB, lanes), axis=0))
+                if k < 3:
+                    moment = moment * doses
+            keep(slot, sums)
+
+    expand([me], [send[me]])
+    group = max(size for size in range(1, GROUP + 1) if (n - 1) % size == 0)
+
+    @pl.loop(0, (n - 1) // group)
+    def _(step):
+        slots = [peer(n - 1 - lax.rem(step * group + at + n // 2 - 1, n - 1)) for at in range(group)]
+        for slot in slots:
+            copy(slot, slot).wait_recv()
+        expand(slots, [recv[slot] for slot in slots])
 
     blocks = n * SUB
     after = (iota((blocks, blocks), 1) > iota((blocks, blocks), 0)).astype(F32).astype(BF16)

time: 27.4 us -> 26 us (0.949)
  Pallas kernels: 26.4 us -> 25 us
    pallas_call x1, Pallas kernels: 24.9 us -> 23.5 us  [body(): pl.pallas_call(functools.partial(kernel, n), out_shape=jax.ShapeDtypeStru...]
where the time goes in v4:
time: 26 us; the launch traced here: 25.7 us
  Pallas kernels  25 us (96%)
  between operations  0.64 us (2%)
    pallas_call x1, Pallas kernels, body(): pl.pallas_call(functools.partial(kernel, n), out_shape=jax.ShapeDtypeStru...  23.5 us
    pallas_call x1, Pallas kernels, body(): pl.pallas_call(functools.partial(unfold, n), out_shape=(out, out), in_spe...  1.53 us

profile of v4, /device:TPU:0, one launch (start us, length us, event | category | flops | bytes accessed | tf_op | source)
XLA Modules:
  0.0 25.7 jit_solution(10490633077301856886)
XLA Ops:
  0.6 23.5 %shard_map.59.held = f32[16,2,128]{2,1,0:T(2,128)} custom-call(s32[1,128]{1,0:T(1,128)} %bitcast.5, bf16[128,2048]{1,0:T(8,128)(2,1)} %dosage_hbm.1, f32[16,128]{1,0:T(8,128)} %bitcast.3, s32[16,128]{1,0:T(8,128)} %bitcast.4), custom_call_target="tpu_custom_call" | custom-call | tf_op jit(solution)/shard_map/pallas_call | solution.py:268
  24.1 1.5 %shard_map.60 = (f32[16,128]{1,0:T(8,128)}, f32[16,128]{1,0:T(8,128)}) custom-call(f32[16,2,128]{2,1,0:T(2,128)} %shard_map.59.held), custom_call_target="tpu_custom_call" | custom-call | tf_op jit(solution)/shard_map/pallas_call | solution.py:293
